TPU v7x, 32 devices: a whole 2x2x4 slice. The times are simulated.
32 devices in a mesh: groups: 2 (over y), slab: 16 (over z, x, core).
Axes of the slice: x: 2, y: 2, z: 4, core: 2. Of those that a mesh axis runs over, the one named last changes fastest.
Arguments:
- rhs: float32 [2, 64, 128, 128], P('groups', 'slab'), parts along dimension 0, may hold values from -6 to 6
- labels: int32 [64, 256, 128], P('slab', 'groups'), parts along dimension 1, may hold values from 0 to 4, as said below
- sigma_table: float32 [5, 3], replicated, may hold values from 0.05 to 2
Outputs:
- correction: float32 [2, 64, 128, 128], P('groups', 'slab'), parts along dimension 0
There are 2 independent parts, one for each index of `groups`. A program takes and returns all parts, laid end to end along the dimension named above; an argument that names none is the same for every part. Nothing has to cross between parts.
Inputs may be any that keep to these rules, and one draw needn't show every extreme that they name: Label 0 marks exactly the voxels outside an ellipsoid centred on the grid with semi-axes 0.45 * 128, 0.45 * 128 and 0.55 * 64 cells; inside, labels 1 to 4 are drawn independently for each voxel.
All inputs are finite; a program needn't handle non-finite values.
Results may differ from a plain program's by a relative error of at most 0.0002.
Values sent between devices are 32-bit elements; how exact they have to be, the bound alone decides.
A program may use at most 64 MiB of HBM per device.

v0:
```python
import jax
import jax.numpy as jnp
from jax import lax
from jax.sharding import PartitionSpec as P

LABELS = 5
OMEGA = 0.8


def extended_2(shard, sides, width):
    for axis, dim in sides:
        size, length = (lax.axis_size(axis), shard.shape[dim])
        up = [(i, (i + 1) % size) for i in range(size - 1)]
        down = [(j, i) for i, j in up]
        last = lax.slice_in_dim(shard, length - width, length, axis=dim)
        first = lax.slice_in_dim(shard, 0, width, axis=dim)
        before = lax.ppermute(last, axis, up)
        after = lax.ppermute(first, axis, down)
        shard = jnp.concatenate([before, shard, after], axis=dim)
    return shard


def harmonic(lower_side, upper_side):
    return 2.0 * lower_side * upper_side / (lower_side + upper_side)


def conductivity(padded, sigma_table, column):
    running = jnp.zeros(padded.shape, jnp.float32)
    for tissue in range(LABELS):
        running = running + jnp.where(padded == tissue, sigma_table[tissue, column], 0.0)
    return running


def coefficients(labels_ext, sigma_table):
    padded = jnp.pad(labels_ext, ((0, 0), (1, 1), (1, 1)))
    active = (padded > 0).astype(jnp.float32)
    sigma_x = conductivity(padded, sigma_table, 0)
    sigma_y = conductivity(padded, sigma_table, 1)
    sigma_z = conductivity(padded, sigma_table, 2)
    inner_x = harmonic(sigma_x[1:-1, :-1, 1:-1], sigma_x[1:-1, 1:, 1:-1])
    couple_x = inner_x * active[1:-1, :-1, 1:-1] * active[1:-1, 1:, 1:-1]
    inner_y = harmonic(sigma_y[1:-1, 1:-1, :-1], sigma_y[1:-1, 1:-1, 1:])
    couple_y = inner_y * active[1:-1, 1:-1, :-1] * active[1:-1, 1:-1, 1:]
    inner_z = harmonic(sigma_z[:-1, 1:-1, 1:-1], sigma_z[1:, 1:-1, 1:-1])
    couple_z = inner_z * active[:-1, 1:-1, 1:-1] * active[1:, 1:-1, 1:-1]
    centre_mask = active[1:-1, 1:-1, 1:-1]
    faces = (
        inner_x[:, :-1]
        + inner_x[:, 1:]
        + inner_y[:, :, :-1]
        + inner_y[:, :, 1:]
        + inner_z[:-1]
        + inner_z[1:]
    )
    diagonal = centre_mask * faces + (1.0 - centre_mask)
    return (centre_mask, diagonal, couple_x, couple_y, couple_z)


def operate(extended, terms):
    couple_x, couple_y, couple_z = (terms[2], terms[3], terms[4])
    centre = extended[:, 1:-1]
    widened = jnp.pad(centre, ((0, 0), (0, 0), (1, 1), (1, 1)))
    neighbours = (
        couple_x[:, :-1] * widened[:, :, :-2, 1:-1] + couple_x[:, 1:] * widened[:, :, 2:, 1:-1]
    )
    neighbours = (
        neighbours
        + couple_y[:, :, :-1] * widened[:, :, 1:-1, :-2]
        + couple_y[:, :, 1:] * widened[:, :, 1:-1, 2:]
    )
    neighbours = neighbours + couple_z[:-1] * extended[:, :-2] + couple_z[1:] * extended[:, 2:]
    return terms[1] * centre - neighbours


def smooth(extended, source, terms):
    image = operate(extended, terms)
    return extended[:, 1:-1] + OMEGA * terms[0] * (source - image) / terms[1]


def start(source, terms):
    return OMEGA * terms[0] * source / terms[1]


def leftover(extended, source, terms):
    return terms[0] * (source - operate(extended, terms))


def pair_matrix(length):
    rows_index = lax.broadcasted_iota(jnp.int32, (length, length // 2), 0)
    cols_index = lax.broadcasted_iota(jnp.int32, (length, length // 2), 1)
    return (rows_index // 2 == cols_index).astype(jnp.float32)


def pair_sum(values, along):
    if along == values.ndim - 1:
        return jnp.matmul(values, pair_matrix(values.shape[-1]), precision=lax.Precision.HIGHEST)
    folded = values.shape[:along] + (values.shape[along] // 2, 2) + values.shape[along + 1 :]
    return jnp.sum(values.reshape(folded), axis=along + 1)


def coarsen(terms):
    centre_mask, diagonal, couple_x, couple_y, couple_z = terms
    coarse_x = pair_sum(pair_sum(couple_x[:, 0::2], 0), 2)
    coarse_y = pair_sum(pair_sum(couple_y[:, :, 0::2], 0), 1)
    coarse_z = pair_sum(pair_sum(couple_z[0::2], 1), 2)
    internal = (
        pair_sum(pair_sum(couple_x[:, 1::2], 0), 2)
        + pair_sum(pair_sum(couple_y[:, :, 1::2], 0), 1)
        + pair_sum(pair_sum(couple_z[1::2], 1), 2)
    )
    counted = pair_sum(pair_sum(pair_sum(centre_mask, 0), 1), 2)
    raw_diag = pair_sum(pair_sum(pair_sum(centre_mask * diagonal, 0), 1), 2) - 2.0 * internal
    coarse_mask = jnp.minimum(counted, 1.0)
    coarse_diag = raw_diag + (1.0 - coarse_mask)
    return ((coarse_mask, coarse_diag, coarse_x, coarse_y, coarse_z), raw_diag)


def restrict(field):
    return pair_sum(pair_sum(pair_sum(field, 1), 2), 3)


def widen(field):
    sides, planes, rows_count, cols_count = field.shape
    spread = pair_matrix(2 * cols_count).T
    along_y = jnp.matmul(field, spread, precision=lax.Precision.HIGHEST)
    grown = jnp.broadcast_to(
        along_y[:, :, None, :, None, :], (sides, planes, 2, rows_count, 2, 2 * cols_count)
    )
    return grown.reshape(sides, 2 * planes, 2 * rows_count, 2 * cols_count)


def plane_total(values):
    return jnp.sum(values, axis=(-2, -1))


def line_terms(coarse_terms, raw_diag):
    line_diag = plane_total(raw_diag) - 2.0 * (
        plane_total(coarse_terms[2]) + plane_total(coarse_terms[3])
    )
    return (line_diag, plane_total(coarse_terms[4]))


def fine_rim(field):
    return extended_2(field, (("slab", 1),), 1)


def coarse_rim(field):
    return extended_2(field, (("slab", 1),), 1)


def on_device(rhs, labels, sigma_table):
    labels_near = extended_2(labels, (("slab", 0),), 1)
    own_terms = coefficients(labels_near, sigma_table)
    source = own_terms[0] * rhs
    fine_first = start(source, own_terms)
    fine_second = smooth(fine_rim(fine_first), source, own_terms)
    fine_left = leftover(fine_rim(fine_second), source, own_terms)
    coarse_terms, raw_diag = coarsen(own_terms)
    coarse_source = restrict(fine_left)
    coarse_first = start(coarse_source, coarse_terms)
    coarse_second = smooth(coarse_rim(coarse_first), coarse_source, coarse_terms)
    coarse_left = leftover(coarse_rim(coarse_second), coarse_source, coarse_terms)
    line_diag, line_faces = line_terms(coarse_terms, raw_diag)
    planes = line_diag.shape[0]
    local_rows = plane_total(coarse_left).T
    band = jnp.stack([line_diag, line_faces[:-1]], axis=1)
    all_rows, all_band = (
        lax.all_gather(local_rows, "slab", axis=0, tiled=True),
        lax.all_gather(band, "slab", axis=0, tiled=True),
    )
    lower_band = -all_band[:, 1]
    upper_band = -jnp.concatenate([all_band[1:, 1], jnp.zeros((1,), jnp.float32)])
    line_solution = lax.linalg.tridiagonal_solve(lower_band, all_band[:, 0], upper_band, all_rows)
    own_line = lax.dynamic_slice_in_dim(line_solution, lax.axis_index("slab") * planes, planes, 0)
    coarse_fix = coarse_second + coarse_terms[0] * own_line.T[:, :, None, None]
    coarse_post = smooth(coarse_rim(coarse_fix), coarse_source, coarse_terms)
    coarse_final = smooth(coarse_rim(coarse_post), coarse_source, coarse_terms)
    fine_third = fine_second + own_terms[0] * widen(coarse_final)
    fine_fourth = smooth(fine_rim(fine_third), source, own_terms)
    return smooth(fine_rim(fine_fourth), source, own_terms)


def solution(mesh):
    placed = (P("groups", "slab", None, None), P("slab", "groups", None), P())
    return jax.shard_map(
        on_device,
        mesh=mesh,
        in_specs=placed,
        out_specs=P("groups", "slab", None, None),
        check_vma=False,
    )
```

profile of v0, /device:TPU:8, one launch (start us, length us, event | category | flops | bytes accessed | tf_op | source)
XLA Modules:
  0.0 265.4 jit_solution(3007158552615316442)
XLA Ops:
  0.0 0.9 fusion.160
  0.9 2.7 %collective-permute-start.1 = (s32[1,128,128]{2,1,0:T(8,128)S(1)}, s32[1,128,128]{2,1,0:T(8,128)S(1)}, u32[]{:S(2)}, u32[]{:S(2)}) collective-permute-start(s32[1,128,128]{2,1,0:T(8,128)S(1)} %get-tuple-element.28), channel_id=1, source_target_pairs={{1,0},{2,1},{3,2},{4,3},{5,4},{6,5},{7,6},{8,7},{9,8},{10,9},{11,1... | collective-permute-start | bytes 196616 | tf_op jit(solution)/shard_map/ppermute | solution.py:18
  3.7 1.9 collective-permute-start
  6.3 0.7 fusion.169
  8.9 1.2 collective-permute-done
  10.5 11.2 %select_add_fusion.2 = (f32[6,130,130]{2,1,0:T(8,128)S(1)}, f32[6,130,130]{2,1,0:T(8,128)}, f32[6,130,130]{2,1,0:T(8,128)S(1)}) fusion(f32[]{:T(128)} %bitcast.6, f32[]{:T(128)} %bitcast.5, f32[]{:T(128)} %bitcast.4, f32[]{:T(128)} %bitcast.3, f32[]{:T(128)} %bitcast.2, s32[6,128,128]{2,1,0:T(8,128)S(1)} %pad_add_fusion, f32[]{:T(128)} %bitcast.16, ...), kind=kLoop, calls=%fused_computation.29 | loop fusion | flops 3244800 | bytes 1610076 | tf_op jit(solution)/shard_map/add | solution.py:30
  22.8 1.7 slice_multiply_fusion.2
  26.2 0.9 bitcast_reduce_fusion.2
  28.0 3.3 %collective-permute-start.3 = (f32[1,1,128,128]{3,2,1,0:T(8,128)}, f32[1,1,128,128]{3,2,1,0:T(8,128)}, u32[]{:S(2)}, u32[]{:S(2)}) collective-permute-start(f32[1,1,128,128]{3,2,1,0:T(8,128)} %get-tuple-element.26), channel_id=1, source_target_pairs={{1,0},{2,1},{3,2},{4,3},{5,4},{6,5},{7,6},{8,7},{9,8},{10,9},{11,1... | collective-permute-start | bytes 196616 | tf_op jit(solution)/shard_map/ppermute | solution.py:18
  31.3 1.9 collective-permute-start.2
  33.2 4.6 %slice.1109 = f32[4,128,64]{2,1,0:T(8,128)S(1)} slice(f32[4,128,129]{2,1,0:T(8,128)S(1)} %get-tuple-element.10), slice={[0:4:1], [0:128:1], [1:129:2]} | slice | bytes 262144 | tf_op jit(solution)/shard_map/slice | solution.py:108
  37.8 0.9 copy-done.6
  39.0 0.7 copy-done.7
  39.8 0.9 copy-done.8
  40.7 0.8 reduce_sum.187
  41.6 0.8 fusion.150
  43.0 0.7 fusion.165
  45.1 0.8 fusion.1
  45.9 4.5 %slice.1116 = f32[4,128,65]{2,1,0:T(8,128)S(1)} slice(f32[4,128,129]{2,1,0:T(8,128)S(1)} %get-tuple-element.10), slice={[0:4:1], [0:128:1], [0:129:2]} | slice | bytes 266240 | tf_op jit(solution)/shard_map/slice | solution.py:104
  50.5 0.7 copy.36
  52.2 1.2 fusion.13
  54.1 4.5 %collective-permute-start.5 = (f32[1,1,128,128]{3,2,1,0:T(8,128)}, f32[1,1,128,128]{3,2,1,0:T(8,128)S(1)}, u32[]{:S(2)}, u32[]{:S(2)}) collective-permute-start(f32[1,1,128,128]{3,2,1,0:T(8,128)} %get-tuple-element.24), channel_id=1, source_target_pairs={{1,0},{2,1},{3,2},{4,3},{5,4},{6,5},{7,6},{8,7},{9,8},{10,9},{11,1... | collective-permute-start | bytes 196616 | tf_op jit(solution)/shard_map/ppermute | solution.py:18
  58.6 1.9 collective-permute-start.4
  60.9 4.4 %collective-permute-done.4 = f32[1,1,128,128]{3,2,1,0:T(8,128)S(1)} collective-permute-done((f32[1,1,128,128]{3,2,1,0:T(8,128)}, f32[1,1,128,128]{3,2,1,0:T(8,128)S(1)}, u32[]{:S(2)}, u32[]{:S(2)}) %collective-permute-start.4) | collective-permute-done | bytes 65568 | tf_op jit(solution)/shard_map/ppermute | solution.py:17
  66.9 15.3 %all-gather.1 = f32[16,2,2]{2,1,0:T(2,128)S(1)} all-gather(f32[1,2,2]{2,1,0:T(2,128)S(1)} %bitcast.570), channel_id=1, replica_groups=mesh['groups'=2,'slab'=16] {'slab'}, dimensions={0}, use_global_device_ids=true | all-gather | bytes 272 | tf_op jit(solution)/shard_map/all_gather | solution.py:169
  83.7 6.0 %collective-permute-start.7 = (f32[1,1,64,64]{3,2,1,0:T(8,128)S(1)}, f32[1,1,64,64]{3,2,1,0:T(8,128)S(1)}, u32[]{:S(2)}, u32[]{:S(2)}) collective-permute-start(f32[1,1,64,64]{3,2,1,0:T(8,128)S(1)} %get-tuple-element.40), channel_id=1, source_target_pairs={{1,0},{2,1},{3,2},{4,3},{5,4},{6,5},{7,6},{8,7},{9,8},{10,9},{11,1... | collective-permute-start | bytes 49160 | tf_op jit(solution)/shard_map/ppermute | solution.py:18
  89.7 1.9 collective-permute-start.6
  91.9 0.7 fusion.172
  92.6 0.7 fusion.170
  93.3 0.7 fusion.175
  94.0 1.8 collective-permute-done.6
  96.0 2.8 %collective-permute-start.9 = (f32[1,1,64,64]{3,2,1,0:T(8,128)S(1)}, f32[1,1,64,64]{3,2,1,0:T(8,128)S(1)}, u32[]{:S(2)}, u32[]{:S(2)}) collective-permute-start(f32[1,1,64,64]{3,2,1,0:T(8,128)S(1)} %get-tuple-element.36), channel_id=1, source_target_pairs={{1,0},{2,1},{3,2},{4,3},{5,4},{6,5},{7,6},{8,7},{9,8},{10,9},{11,1... | collective-permute-start | bytes 49160 | tf_op jit(solution)/shard_map/ppermute | solution.py:18
  98.7 2.1 collective-permute-start.8
  160.8 24.9 %all-reduce.9 = f32[32]{0:T(128)S(1)} all-reduce(f32[32]{0:T(128)S(1)} %dynamic-update-slice), channel_id=2, replica_groups=mesh['groups'=2,'slab'=16] {'slab'}, use_global_device_ids=true, to_apply=%add.9 | all-reduce | flops 32 | bytes 256
  186.4 0.7 fusion.171
  228.9 1.9 collective-permute-start.11
  230.8 2.4 collective-permute-start.10
  233.2 3.7 %collective-permute-done.10 = f32[1,1,64,64]{3,2,1,0:T(8,128)S(1)} collective-permute-done((f32[1,1,64,64]{3,2,1,0:T(8,128)S(1)}, f32[1,1,64,64]{3,2,1,0:T(8,128)S(1)}, u32[]{:S(2)}, u32[]{:S(2)}) %collective-permute-start.10) | collective-permute-done | bytes 16416 | tf_op jit(solution)/shard_map/ppermute | solution.py:17
  237.1 2.7 %collective-permute-start.13 = (f32[1,1,64,64]{3,2,1,0:T(8,128)S(1)}, f32[1,1,64,64]{3,2,1,0:T(8,128)S(1)}, u32[]{:S(2)}, u32[]{:S(2)}) collective-permute-start(f32[1,1,64,64]{3,2,1,0:T(8,128)S(1)} %get-tuple-element.30), channel_id=1, source_target_pairs={{1,0},{2,1},{3,2},{4,3},{5,4},{6,5},{7,6},{8,7},{9,8},{10,9},{11,1... | collective-permute-start | bytes 49160 | tf_op jit(solution)/shard_map/ppermute | solution.py:18
  239.8 1.9 collective-permute-start.12
  241.7 4.8 %collective-permute-done.12 = f32[1,1,64,64]{3,2,1,0:T(8,128)S(1)} collective-permute-done((f32[1,1,64,64]{3,2,1,0:T(8,128)S(1)}, f32[1,1,64,64]{3,2,1,0:T(8,128)S(1)}, u32[]{:S(2)}, u32[]{:S(2)}) %collective-permute-start.12) | collective-permute-done | bytes 16416 | tf_op jit(solution)/shard_map/ppermute | solution.py:17
  247.1 1.9 collective-permute-start.15
  249.0 2.4 collective-permute-start.14
  251.4 4.1 %collective-permute-done.14 = f32[1,1,128,128]{3,2,1,0:T(8,128)S(1)} collective-permute-done((f32[1,1,128,128]{3,2,1,0:T(8,128)S(1)}, f32[1,1,128,128]{3,2,1,0:T(8,128)S(1)}, u32[]{:S(2)}, u32[]{:S(2)}) %collective-permute-start.14) | collective-permute-done | bytes 65568 | tf_op jit(solution)/shard_map/ppermute | solution.py:17
  255.9 1.9 collective-permute-start.17
  257.9 2.4 collective-permute-start.16
  260.3 4.1 %collective-permute-done.16 = f32[1,1,128,128]{3,2,1,0:T(8,128)S(1)} collective-permute-done((f32[1,1,128,128]{3,2,1,0:T(8,128)S(1)}, f32[1,1,128,128]{3,2,1,0:T(8,128)S(1)}, u32[]{:S(2)}, u32[]{:S(2)}) %collective-permute-start.16) | collective-permute-done | bytes 65568 | tf_op jit(solution)/shard_map/ppermute | solution.py:17
  264.4 1.1 fusion.53
  (108 shorter events, 16.9 us)
Async XLA Ops:
  0.0 10.1 %copy-start.4 = (s32[4,128,128]{2,1,0:T(8,128)S(1)}, s32[4,128,128]{2,1,0:T(8,128)}, u32[]{:S(2)}) copy-start(s32[4,128,128]{2,1,0:T(8,128)} %param.4) | copy-start | bytes 786436
  0.9 8.0 %collective-permute-start.1 = (s32[1,128,128]{2,1,0:T(8,128)S(1)}, s32[1,128,128]{2,1,0:T(8,128)S(1)}, u32[]{:S(2)}, u32[]{:S(2)}) collective-permute-start(s32[1,128,128]{2,1,0:T(8,128)S(1)} %get-tuple-element.28), channel_id=1, source_target_pairs={{1,0},{2,1},{3,2},{4,3},{5,4},{6,5},{7,6},{8,7},{9,8},{10,9},{11,1... | collective-permute-start | bytes 196616 | tf_op jit(solution)/shard_map/ppermute | solution.py:18
  3.7 6.5 %collective-permute-start = (s32[1,128,128]{2,1,0:T(8,128)S(1)}, s32[1,128,128]{2,1,0:T(8,128)S(1)}, u32[]{:S(2)}, u32[]{:S(2)}) collective-permute-start(s32[1,128,128]{2,1,0:T(8,128)S(1)} %get-tuple-element.27), channel_id=1, source_target_pairs={{0,1},{1,2},{2,3},{3,4},{4,5},{5,6},{6,7},{7,8},{8,9},{9,10},{10,1... | collective-permute-start | bytes 196616 | tf_op jit(solution)/shard_map/ppermute | solution.py:17
  5.6 0.7 copy-start.14
  7.0 0.7 copy-start.15
  26.2 1.0 copy-start.9
  28.0 24.2 %collective-permute-start.3 = (f32[1,1,128,128]{3,2,1,0:T(8,128)}, f32[1,1,128,128]{3,2,1,0:T(8,128)}, u32[]{:S(2)}, u32[]{:S(2)}) collective-permute-start(f32[1,1,128,128]{3,2,1,0:T(8,128)} %get-tuple-element.26), channel_id=1, source_target_pairs={{1,0},{2,1},{3,2},{4,3},{5,4},{6,5},{7,6},{8,7},{9,8},{10,9},{11,1... | collective-permute-start | bytes 196616 | tf_op jit(solution)/shard_map/ppermute | solution.py:18
  31.3 20.9 %collective-permute-start.2 = (f32[1,1,128,128]{3,2,1,0:T(8,128)}, f32[1,1,128,128]{3,2,1,0:T(8,128)}, u32[]{:S(2)}, u32[]{:S(2)}) collective-permute-start(f32[1,1,128,128]{3,2,1,0:T(8,128)} %get-tuple-element.25), channel_id=1, source_target_pairs={{0,1},{1,2},{2,3},{3,4},{4,5},{5,6},{6,7},{7,8},{8,9},{9,10},{10,1... | collective-permute-start | bytes 196616 | tf_op jit(solution)/shard_map/ppermute | solution.py:17
  37.8 0.9 copy-start.6
  38.8 0.9 copy-start.7
  39.8 0.9 copy-start.8
  39.8 1.7 copy-start.5
  42.6 1.1 copy-start.3
  44.2 0.8 copy-start.10
  44.2 0.9 copy-start.11
  45.9 4.6 %copy-start.13 = (f32[2,64,64]{1,2,0:T(8,128)S(1)}, f32[2,64,64]{1,2,0:T(8,128)}, u32[]{:S(2)}) copy-start(f32[2,64,64]{1,2,0:T(8,128)} %get-tuple-element.38) | copy-start | bytes 98308
  50.5 0.8 copy-start.12
  54.1 6.9 %collective-permute-start.5 = (f32[1,1,128,128]{3,2,1,0:T(8,128)}, f32[1,1,128,128]{3,2,1,0:T(8,128)S(1)}, u32[]{:S(2)}, u32[]{:S(2)}) collective-permute-start(f32[1,1,128,128]{3,2,1,0:T(8,128)} %get-tuple-element.24), channel_id=1, source_target_pairs={{1,0},{2,1},{3,2},{4,3},{5,4},{6,5},{7,6},{8,7},{9,8},{10,9},{11,1... | collective-permute-start | bytes 196616 | tf_op jit(solution)/shard_map/ppermute | solution.py:18
  58.6 6.7 %collective-permute-start.4 = (f32[1,1,128,128]{3,2,1,0:T(8,128)}, f32[1,1,128,128]{3,2,1,0:T(8,128)S(1)}, u32[]{:S(2)}, u32[]{:S(2)}) collective-permute-start(f32[1,1,128,128]{3,2,1,0:T(8,128)} %get-tuple-element.23), channel_id=1, source_target_pairs={{0,1},{1,2},{2,3},{3,4},{4,5},{5,6},{6,7},{7,8},{8,9},{9,10},{10,1... | collective-permute-start | bytes 196616 | tf_op jit(solution)/shard_map/ppermute | solution.py:17
  65.8 0.8 copy-start
  83.6 12.2 %copy-start.2 = (f32[2,64,64]{2,1,0:T(8,128)S(1)}, f32[2,64,64]{2,1,0:T(8,128)}, u32[]{:S(2)}) copy-start(f32[2,64,64]{2,1,0:T(8,128)} %copy.35) | copy-start | bytes 98308
  83.7 12.2 %copy-start.1 = (f32[2,64,64]{2,1,0:T(8,128)S(1)}, f32[2,64,64]{2,1,0:T(8,128)}, u32[]{:S(2)}) copy-start(f32[2,64,64]{2,1,0:T(8,128)} %copy.36) | copy-start | bytes 98308
  83.7 10.4 %collective-permute-start.7 = (f32[1,1,64,64]{3,2,1,0:T(8,128)S(1)}, f32[1,1,64,64]{3,2,1,0:T(8,128)S(1)}, u32[]{:S(2)}, u32[]{:S(2)}) collective-permute-start(f32[1,1,64,64]{3,2,1,0:T(8,128)S(1)} %get-tuple-element.40), channel_id=1, source_target_pairs={{1,0},{2,1},{3,2},{4,3},{5,4},{6,5},{7,6},{8,7},{9,8},{10,9},{11,1... | collective-permute-start | bytes 49160 | tf_op jit(solution)/shard_map/ppermute | solution.py:18
  89.7 6.1 %collective-permute-start.6 = (f32[1,1,64,64]{3,2,1,0:T(8,128)S(1)}, f32[1,1,64,64]{3,2,1,0:T(8,128)S(1)}, u32[]{:S(2)}, u32[]{:S(2)}) collective-permute-start(f32[1,1,64,64]{3,2,1,0:T(8,128)S(1)} %get-tuple-element.39), channel_id=1, source_target_pairs={{0,1},{1,2},{2,3},{3,4},{4,5},{5,6},{6,7},{7,8},{8,9},{9,10},{10,1... | collective-permute-start | bytes 49160 | tf_op jit(solution)/shard_map/ppermute | solution.py:17
  96.0 64.4 %collective-permute-start.9 = (f32[1,1,64,64]{3,2,1,0:T(8,128)S(1)}, f32[1,1,64,64]{3,2,1,0:T(8,128)S(1)}, u32[]{:S(2)}, u32[]{:S(2)}) collective-permute-start(f32[1,1,64,64]{3,2,1,0:T(8,128)S(1)} %get-tuple-element.36), channel_id=1, source_target_pairs={{1,0},{2,1},{3,2},{4,3},{5,4},{6,5},{7,6},{8,7},{9,8},{10,9},{11,1... | collective-permute-start | bytes 49160 | tf_op jit(solution)/shard_map/ppermute | solution.py:18
  98.7 61.6 %collective-permute-start.8 = (f32[1,1,64,64]{3,2,1,0:T(8,128)S(1)}, f32[1,1,64,64]{3,2,1,0:T(8,128)S(1)}, u32[]{:S(2)}, u32[]{:S(2)}) collective-permute-start(f32[1,1,64,64]{3,2,1,0:T(8,128)S(1)} %get-tuple-element.35), channel_id=1, source_target_pairs={{0,1},{1,2},{2,3},{3,4},{4,5},{5,6},{6,7},{7,8},{8,9},{9,10},{10,1... | collective-permute-start | bytes 49160 | tf_op jit(solution)/shard_map/ppermute | solution.py:17
  228.9 4.3 %collective-permute-start.11 = (f32[1,1,64,64]{3,2,1,0:T(8,128)S(1)}, f32[1,1,64,64]{3,2,1,0:T(8,128)S(1)}, u32[]{:S(2)}, u32[]{:S(2)}) collective-permute-start(f32[1,1,64,64]{3,2,1,0:T(8,128)S(1)} %get-tuple-element.32), channel_id=1, source_target_pairs={{1,0},{2,1},{3,2},{4,3},{5,4},{6,5},{7,6},{8,7},{9,8},{10,9},{11,1... | collective-permute-start | bytes 49160 | tf_op jit(solution)/shard_map/ppermute | solution.py:18
  230.8 6.1 %collective-permute-start.10 = (f32[1,1,64,64]{3,2,1,0:T(8,128)S(1)}, f32[1,1,64,64]{3,2,1,0:T(8,128)S(1)}, u32[]{:S(2)}, u32[]{:S(2)}) collective-permute-start(f32[1,1,64,64]{3,2,1,0:T(8,128)S(1)} %get-tuple-element.31), channel_id=1, source_target_pairs={{0,1},{1,2},{2,3},{3,4},{4,5},{5,6},{6,7},{7,8},{8,9},{9,10},{10,1... | collective-permute-start | bytes 49160 | tf_op jit(solution)/shard_map/ppermute | solution.py:17
  237.1 4.6 %collective-permute-start.13 = (f32[1,1,64,64]{3,2,1,0:T(8,128)S(1)}, f32[1,1,64,64]{3,2,1,0:T(8,128)S(1)}, u32[]{:S(2)}, u32[]{:S(2)}) collective-permute-start(f32[1,1,64,64]{3,2,1,0:T(8,128)S(1)} %get-tuple-element.30), channel_id=1, source_target_pairs={{1,0},{2,1},{3,2},{4,3},{5,4},{6,5},{7,6},{8,7},{9,8},{10,9},{11,1... | collective-permute-start | bytes 49160 | tf_op jit(solution)/shard_map/ppermute | solution.py:18
  239.8 6.8 %collective-permute-start.12 = (f32[1,1,64,64]{3,2,1,0:T(8,128)S(1)}, f32[1,1,64,64]{3,2,1,0:T(8,128)S(1)}, u32[]{:S(2)}, u32[]{:S(2)}) collective-permute-start(f32[1,1,64,64]{3,2,1,0:T(8,128)S(1)} %get-tuple-element.29), channel_id=1, source_target_pairs={{0,1},{1,2},{2,3},{3,4},{4,5},{5,6},{6,7},{7,8},{8,9},{9,10},{10,1... | collective-permute-start | bytes 49160 | tf_op jit(solution)/shard_map/ppermute | solution.py:17
  247.1 4.3 %collective-permute-start.15 = (f32[1,1,128,128]{3,2,1,0:T(8,128)S(1)}, f32[1,1,128,128]{3,2,1,0:T(8,128)S(1)}, u32[]{:S(2)}, u32[]{:S(2)}) collective-permute-start(f32[1,1,128,128]{3,2,1,0:T(8,128)S(1)} %get-tuple-element.22), channel_id=1, source_target_pairs={{1,0},{2,1},{3,2},{4,3},{5,4},{6,5},{7,6},{8,7},{9,8},{10,9},{11,1... | collective-permute-start | bytes 196616 | tf_op jit(solution)/shard_map/ppermute | solution.py:18
  249.0 6.5 %collective-permute-start.14 = (f32[1,1,128,128]{3,2,1,0:T(8,128)S(1)}, f32[1,1,128,128]{3,2,1,0:T(8,128)S(1)}, u32[]{:S(2)}, u32[]{:S(2)}) collective-permute-start(f32[1,1,128,128]{3,2,1,0:T(8,128)S(1)} %get-tuple-element.21), channel_id=1, source_target_pairs={{0,1},{1,2},{2,3},{3,4},{4,5},{5,6},{6,7},{7,8},{8,9},{9,10},{10,1... | collective-permute-start | bytes 196616 | tf_op jit(solution)/shard_map/ppermute | solution.py:17
  255.9 4.3 %collective-permute-start.17 = (f32[1,1,128,128]{3,2,1,0:T(8,128)S(1)}, f32[1,1,128,128]{3,2,1,0:T(8,128)S(1)}, u32[]{:S(2)}, u32[]{:S(2)}) collective-permute-start(f32[1,1,128,128]{3,2,1,0:T(8,128)S(1)} %get-tuple-element.20), channel_id=1, source_target_pairs={{1,0},{2,1},{3,2},{4,3},{5,4},{6,5},{7,6},{8,7},{9,8},{10,9},{11,1... | collective-permute-start | bytes 196616 | tf_op jit(solution)/shard_map/ppermute | solution.py:18
  257.9 6.5 %collective-permute-start.16 = (f32[1,1,128,128]{3,2,1,0:T(8,128)S(1)}, f32[1,1,128,128]{3,2,1,0:T(8,128)S(1)}, u32[]{:S(2)}, u32[]{:S(2)}) collective-permute-start(f32[1,1,128,128]{3,2,1,0:T(8,128)S(1)} %get-tuple-element.19), channel_id=1, source_target_pairs={{0,1},{1,2},{2,3},{3,4},{4,5},{5,6},{6,7},{7,8},{8,9},{9,10},{10,1... | collective-permute-start | bytes 196616 | tf_op jit(solution)/shard_map/ppermute | solution.py:17
where the time goes:
time: 268 us; the launch traced here: 265 us
  between operations  101 us (38%)
  starting transfers between devices  46.7 us (17%)
  blocking collectives  40.2 us (15%)
  local copies, waits for them, and re-layouts  28.7 us (11%)
  waiting for transfers between devices  24.1 us (9%)
  other arithmetic  21.2 us (8%)
  matrix products  3.07 us (1%)
    ppermute x9, starting transfers between devices, extended_2(): after = lax.ppermute(first, axis, down)  27.8 us
    unnamed x1, blocking collectives  24.9 us
    ppermute x9, waiting for transfers between devices, extended_2(): before = lax.ppermute(last, axis, up)  24.1 us
    ppermute x9, starting transfers between devices, extended_2(): before = lax.ppermute(last, axis, up)  18.9 us
    all_gather x1, blocking collectives, on_device(): lax.all_gather(band, 'slab', axis=0, tiled=True)  15.3 us
    add x1, other arithmetic, conductivity(): running + jnp.where(padded == tissue, sigma_table[tissue, column], 0.0)  11.2 us
    unnamed x39, local copies, waits for them, and re-layouts  7.66 us
    slice x8, local copies, waits for them, and re-layouts, on_device(): lax.linalg.tridiagonal_solve(lower_band, all_band[:, 0], upper_band, all_...  5.56 us
  transfers between devices with their start and end apart: 18, of which 7 were waited for; matrix products, arithmetic and copies ran while one was open for 8% of the time, Pallas kernels for 0%

commit v1 on v0

--- a/solution.py
+++ b/solution.py
@@ -2,6 +2,7 @@
 import jax.numpy as jnp
 from jax import lax
 from jax.sharding import PartitionSpec as P
+from jax.lax import axis_index, ppermute, psum
 
 LABELS = 5
 OMEGA = 0.8
@@ -164,9 +165,24 @@
     planes = line_diag.shape[0]
     local_rows = plane_total(coarse_left).T
     band = jnp.stack([line_diag, line_faces[:-1]], axis=1)
+
+    def sample_update(field_in, peer_axis, where_dim):
+        d_next, t_next = (psum(1, axis_name=peer_axis), axis_index(peer_axis))
+        top, k_now = (field_in, 1)
+        while k_now < d_next:
+            items = []
+            for d in range(d_next):
+                items.append((d, d ^ k_now))
+            val2 = ppermute(top, axis_name=peer_axis, perm=items)
+            q_next = jnp.concatenate([top, val2], where_dim)
+            opened = jnp.concatenate([val2, top], axis=where_dim)
+            top = jnp.where(t_next & k_now == 0, q_next, opened)
+            k_now = 2 * k_now
+        return top
+
     all_rows, all_band = (
         lax.all_gather(local_rows, "slab", axis=0, tiled=True),
-        lax.all_gather(band, "slab", axis=0, tiled=True),
+        sample_update(band, "slab", where_dim=0),
     )
     lower_band = -all_band[:, 1]
     upper_band = -jnp.concatenate([all_band[1:, 1], jnp.zeros((1,), jnp.float32)])

time: 268 us -> 258 us (0.963)
  blocking collectives: 40.2 us -> 24.9 us
  waiting for transfers between devices: 24.1 us -> 28.9 us
    all_gather x1 -> x0, blocking collectives: 15.3 us -> none  [on_device(): lax.all_gather(band, 'slab', axis=0, tiled=True)]
    ppermute x0 -> x4, waiting for transfers between devices: none -> 6.23 us  [sample_update(): val2 = ppermute(top, axis_name=peer_axis, perm=items)]
    ppermute x9, starting transfers between devices: 27.8 us -> 25.1 us  [extended_2(): after = lax.ppermute(first, axis, down)]
    unnamed x39 -> x37, local copies, waits for them, and re-layouts: 7.66 us -> 7.56 us
  transfers between devices with their start and end apart: 18 -> 22, of which waited for: 7 -> 10; matrix products, arithmetic and copies ran while one was open for 8% -> 9% of each run, Pallas kernels for 0% -> 0%
where the time goes in v1:
time: 258 us; the launch traced here: 255 us
  between operations  101 us (39%)
  starting transfers between devices  46.7 us (18%)
  waiting for transfers between devices  28.9 us (11%)
  local copies, waits for them, and re-layouts  28.6 us (11%)
  blocking collectives  24.9 us (10%)
  other arithmetic  21.6 us (8%)
  matrix products  3.07 us (1%)
    ppermute x9, starting transfers between devices, extended_2(): after = lax.ppermute(first, axis, down)  25.1 us
    unnamed x1, blocking collectives  24.9 us
    ppermute x9, waiting for transfers between devices, extended_2(): before = lax.ppermute(last, axis, up)  22.6 us
    ppermute x9, starting transfers between devices, extended_2(): before = lax.ppermute(last, axis, up)  18.9 us
    add x1, other arithmetic, conductivity(): running + jnp.where(padded == tissue, sigma_table[tissue, column], 0.0)  11.3 us
    unnamed x37, local copies, waits for them, and re-layouts  7.56 us
    ppermute x4, waiting for transfers between devices, sample_update(): val2 = ppermute(top, axis_name=peer_axis, perm=items)  6.23 us
    slice x8, local copies, waits for them, and re-layouts, on_device(): lax.linalg.tridiagonal_solve(lower_band, all_band[:, 0], upper_band, all_...  5.72 us
  transfers between devices with their start and end apart: 22, of which 10 were waited for; matrix products, arithmetic and copies ran while one was open for 9% of the time, Pallas kernels for 0%

profile of v1, /device:TPU:8, one launch (start us, length us, event | category | flops | bytes accessed | tf_op | source)
XLA Modules:
  0.0 255.1 jit_solution(1266777987635483454)
XLA Ops:
  0.0 0.9 fusion.160
  0.9 2.7 %collective-permute-start.1 = (s32[1,128,128]{2,1,0:T(8,128)S(1)}, s32[1,128,128]{2,1,0:T(8,128)S(1)}, u32[]{:S(2)}, u32[]{:S(2)}) collective-permute-start(s32[1,128,128]{2,1,0:T(8,128)S(1)} %get-tuple-element.28), channel_id=1, source_target_pairs={{1,0},{2,1},{3,2},{4,3},{5,4},{6,5},{7,6},{8,7},{9,8},{10,9},{11,1... | collective-permute-start | bytes 196616 | tf_op jit(solution)/shard_map/ppermute | solution.py:19
  3.7 1.9 collective-permute-start
  9.0 1.1 collective-permute-done
  10.5 11.3 %select_add_fusion.2 = (f32[6,130,130]{2,1,0:T(8,128)S(1)}, f32[6,130,130]{2,1,0:T(8,128)}, f32[6,130,130]{2,1,0:T(8,128)S(1)}) fusion(f32[]{:T(128)} %bitcast.6, f32[]{:T(128)} %bitcast.5, f32[]{:T(128)} %bitcast.4, f32[]{:T(128)} %bitcast.3, f32[]{:T(128)} %bitcast.2, s32[6,128,128]{2,1,0:T(8,128)S(1)} %pad_add_fusion, f32[]{:T(128)} %bitcast.16, ...), kind=kLoop, calls=%fused_computation.29 | loop fusion | flops 3244800 | bytes 1610076 | tf_op jit(solution)/shard_map/add | solution.py:31
  22.8 1.7 slice_multiply_fusion.2
  26.3 0.9 bitcast_reduce_fusion.2
  28.1 3.4 %collective-permute-start.3 = (f32[1,1,128,128]{3,2,1,0:T(8,128)}, f32[1,1,128,128]{3,2,1,0:T(8,128)}, u32[]{:S(2)}, u32[]{:S(2)}) collective-permute-start(f32[1,1,128,128]{3,2,1,0:T(8,128)} %get-tuple-element.26), channel_id=1, source_target_pairs={{1,0},{2,1},{3,2},{4,3},{5,4},{6,5},{7,6},{8,7},{9,8},{10,9},{11,1... | collective-permute-start | bytes 196616 | tf_op jit(solution)/shard_map/ppermute | solution.py:19
  31.5 1.9 collective-permute-start.2
  33.4 4.6 %slice.1109 = f32[4,128,64]{2,1,0:T(8,128)S(1)} slice(f32[4,128,129]{2,1,0:T(8,128)S(1)} %get-tuple-element.10), slice={[0:4:1], [0:128:1], [1:129:2]} | slice | bytes 262144 | tf_op jit(solution)/shard_map/slice | solution.py:109
  38.0 0.9 copy-done.6
  39.2 0.7 copy-done.7
  40.0 0.9 copy-done.8
  40.9 0.8 reduce_sum.187
  41.8 0.8 fusion.150
  43.2 0.7 fusion.165
  45.3 0.8 fusion.1
  46.1 4.5 %slice.1116 = f32[4,128,65]{2,1,0:T(8,128)S(1)} slice(f32[4,128,129]{2,1,0:T(8,128)S(1)} %get-tuple-element.10), slice={[0:4:1], [0:128:1], [0:129:2]} | slice | bytes 266240 | tf_op jit(solution)/shard_map/slice | solution.py:105
  52.4 1.2 fusion.13
  54.3 4.5 %collective-permute-start.5 = (f32[1,1,128,128]{3,2,1,0:T(8,128)}, f32[1,1,128,128]{3,2,1,0:T(8,128)S(1)}, u32[]{:S(2)}, u32[]{:S(2)}) collective-permute-start(f32[1,1,128,128]{3,2,1,0:T(8,128)} %get-tuple-element.24), channel_id=1, source_target_pairs={{1,0},{2,1},{3,2},{4,3},{5,4},{6,5},{7,6},{8,7},{9,8},{10,9},{11,1... | collective-permute-start | bytes 196616 | tf_op jit(solution)/shard_map/ppermute | solution.py:19
  58.8 1.9 collective-permute-start.4
  61.1 4.4 %collective-permute-done.4 = f32[1,1,128,128]{3,2,1,0:T(8,128)S(1)} collective-permute-done((f32[1,1,128,128]{3,2,1,0:T(8,128)}, f32[1,1,128,128]{3,2,1,0:T(8,128)S(1)}, u32[]{:S(2)}, u32[]{:S(2)}) %collective-permute-start.4) | collective-permute-done | bytes 65568 | tf_op jit(solution)/shard_map/ppermute | solution.py:18
  67.1 1.1 collective-permute-done.10
  68.3 3.6 %collective-permute-done.11 = f32[4,2]{0,1:T(2,128)S(1)} collective-permute-done((f32[4,2]{0,1:T(2,128)S(1)}, f32[4,2]{0,1:T(2,128)S(1)}, u32[]{:S(2)}, u32[]{:S(2)}) %collective-permute-start.11) | collective-permute-done | bytes 64 | tf_op jit(solution)/shard_map/ppermute | solution.py:176
  72.0 2.0 collective-permute-start.7
  74.0 1.6 collective-permute-done.12
  75.6 2.6 %collective-permute-start.13 = (f32[16,2]{0,1:T(2,128)S(1)}, f32[16,2]{0,1:T(2,128)S(1)}, u32[]{:S(2)}, u32[]{:S(2)}) collective-permute-start(f32[16,2]{0,1:T(2,128)S(1)} %maximum_select_fusion.2), channel_id=1, source_target_pairs={{0,8},{1,9},{2,10},{3,11},{4,12},{5,13},{6,14},{7,15},{8,0},{9,1},... | collective-permute-start | bytes 392 | tf_op jit(solution)/shard_map/ppermute | solution.py:176
  78.2 1.9 collective-permute-start.6
  81.0 0.7 fusion.168
  81.8 0.7 fusion.172
  82.5 0.7 fusion.170
  84.5 4.2 %collective-permute-start.9 = (f32[1,1,64,64]{3,2,1,0:T(8,128)S(1)}, f32[1,1,64,64]{3,2,1,0:T(8,128)S(1)}, u32[]{:S(2)}, u32[]{:S(2)}) collective-permute-start(f32[1,1,64,64]{3,2,1,0:T(8,128)S(1)} %get-tuple-element.36), channel_id=1, source_target_pairs={{1,0},{2,1},{3,2},{4,3},{5,4},{6,5},{7,6},{8,7},{9,8},{10,9},{11,1... | collective-permute-start | bytes 49160 | tf_op jit(solution)/shard_map/ppermute | solution.py:19
  88.7 2.1 collective-permute-start.8
  150.8 24.9 %all-reduce.9 = f32[32]{0:T(128)S(1)} all-reduce(f32[32]{0:T(128)S(1)} %dynamic-update-slice), channel_id=2, replica_groups=mesh['groups'=2,'slab'=16] {'slab'}, use_global_device_ids=true, to_apply=%add.9 | all-reduce | flops 32 | bytes 256
  176.4 0.7 fusion.171
  218.7 1.9 collective-permute-start.15
  220.6 2.4 collective-permute-start.14
  223.1 3.7 %collective-permute-done.14 = f32[1,1,64,64]{3,2,1,0:T(8,128)S(1)} collective-permute-done((f32[1,1,64,64]{3,2,1,0:T(8,128)S(1)}, f32[1,1,64,64]{3,2,1,0:T(8,128)S(1)}, u32[]{:S(2)}, u32[]{:S(2)}) %collective-permute-start.14) | collective-permute-done | bytes 16416 | tf_op jit(solution)/shard_map/ppermute | solution.py:18
  226.9 2.4 collective-permute-start.17
  229.4 1.9 collective-permute-start.16
  231.3 4.9 %collective-permute-done.16 = f32[1,1,64,64]{3,2,1,0:T(8,128)S(1)} collective-permute-done((f32[1,1,64,64]{3,2,1,0:T(8,128)S(1)}, f32[1,1,64,64]{3,2,1,0:T(8,128)S(1)}, u32[]{:S(2)}, u32[]{:S(2)}) %collective-permute-start.16) | collective-permute-done | bytes 16416 | tf_op jit(solution)/shard_map/ppermute | solution.py:18
  236.7 1.9 collective-permute-start.19
  238.7 2.4 collective-permute-start.18
  241.1 4.1 %collective-permute-done.18 = f32[1,1,128,128]{3,2,1,0:T(8,128)S(1)} collective-permute-done((f32[1,1,128,128]{3,2,1,0:T(8,128)S(1)}, f32[1,1,128,128]{3,2,1,0:T(8,128)S(1)}, u32[]{:S(2)}, u32[]{:S(2)}) %collective-permute-start.18) | collective-permute-done | bytes 65568 | tf_op jit(solution)/shard_map/ppermute | solution.py:18
  245.6 1.9 collective-permute-start.21
  247.5 2.4 collective-permute-start.20
  250.0 4.1 %collective-permute-done.20 = f32[1,1,128,128]{3,2,1,0:T(8,128)S(1)} collective-permute-done((f32[1,1,128,128]{3,2,1,0:T(8,128)S(1)}, f32[1,1,128,128]{3,2,1,0:T(8,128)S(1)}, u32[]{:S(2)}, u32[]{:S(2)}) %collective-permute-start.20) | collective-permute-done | bytes 65568 | tf_op jit(solution)/shard_map/ppermute | solution.py:18
  254.0 1.1 fusion.53
  (115 shorter events, 19.0 us)
Async XLA Ops:
  0.0 10.1 %copy-start.4 = (s32[4,128,128]{2,1,0:T(8,128)S(1)}, s32[4,128,128]{2,1,0:T(8,128)}, u32[]{:S(2)}) copy-start(s32[4,128,128]{2,1,0:T(8,128)} %param.4) | copy-start | bytes 786436
  0.9 8.1 %collective-permute-start.1 = (s32[1,128,128]{2,1,0:T(8,128)S(1)}, s32[1,128,128]{2,1,0:T(8,128)S(1)}, u32[]{:S(2)}, u32[]{:S(2)}) collective-permute-start(s32[1,128,128]{2,1,0:T(8,128)S(1)} %get-tuple-element.28), channel_id=1, source_target_pairs={{1,0},{2,1},{3,2},{4,3},{5,4},{6,5},{7,6},{8,7},{9,8},{10,9},{11,1... | collective-permute-start | bytes 196616 | tf_op jit(solution)/shard_map/ppermute | solution.py:19
  3.7 6.5 %collective-permute-start = (s32[1,128,128]{2,1,0:T(8,128)S(1)}, s32[1,128,128]{2,1,0:T(8,128)S(1)}, u32[]{:S(2)}, u32[]{:S(2)}) collective-permute-start(s32[1,128,128]{2,1,0:T(8,128)S(1)} %get-tuple-element.27), channel_id=1, source_target_pairs={{0,1},{1,2},{2,3},{3,4},{4,5},{5,6},{6,7},{7,8},{8,9},{9,10},{10,1... | collective-permute-start | bytes 196616 | tf_op jit(solution)/shard_map/ppermute | solution.py:18
  5.6 0.7 copy-start.14
  7.0 0.7 copy-start.15
  26.3 1.0 copy-start.9
  28.1 24.3 %collective-permute-start.3 = (f32[1,1,128,128]{3,2,1,0:T(8,128)}, f32[1,1,128,128]{3,2,1,0:T(8,128)}, u32[]{:S(2)}, u32[]{:S(2)}) collective-permute-start(f32[1,1,128,128]{3,2,1,0:T(8,128)} %get-tuple-element.26), channel_id=1, source_target_pairs={{1,0},{2,1},{3,2},{4,3},{5,4},{6,5},{7,6},{8,7},{9,8},{10,9},{11,1... | collective-permute-start | bytes 196616 | tf_op jit(solution)/shard_map/ppermute | solution.py:19
  31.5 20.9 %collective-permute-start.2 = (f32[1,1,128,128]{3,2,1,0:T(8,128)}, f32[1,1,128,128]{3,2,1,0:T(8,128)}, u32[]{:S(2)}, u32[]{:S(2)}) collective-permute-start(f32[1,1,128,128]{3,2,1,0:T(8,128)} %get-tuple-element.25), channel_id=1, source_target_pairs={{0,1},{1,2},{2,3},{3,4},{4,5},{5,6},{6,7},{7,8},{8,9},{9,10},{10,1... | collective-permute-start | bytes 196616 | tf_op jit(solution)/shard_map/ppermute | solution.py:18
  38.0 0.9 copy-start.6
  39.0 0.9 copy-start.7
  40.0 0.9 copy-start.8
  40.0 1.7 copy-start.5
  42.8 1.1 copy-start.3
  44.4 0.8 copy-start.10
  44.4 0.9 copy-start.11
  46.1 4.6 %copy-start.13 = (f32[2,64,64]{1,2,0:T(8,128)S(1)}, f32[2,64,64]{1,2,0:T(8,128)}, u32[]{:S(2)}) copy-start(f32[2,64,64]{1,2,0:T(8,128)} %get-tuple-element.38) | copy-start | bytes 98308
  50.7 0.8 copy-start.12
  54.3 6.9 %collective-permute-start.5 = (f32[1,1,128,128]{3,2,1,0:T(8,128)}, f32[1,1,128,128]{3,2,1,0:T(8,128)S(1)}, u32[]{:S(2)}, u32[]{:S(2)}) collective-permute-start(f32[1,1,128,128]{3,2,1,0:T(8,128)} %get-tuple-element.24), channel_id=1, source_target_pairs={{1,0},{2,1},{3,2},{4,3},{5,4},{6,5},{7,6},{8,7},{9,8},{10,9},{11,1... | collective-permute-start | bytes 196616 | tf_op jit(solution)/shard_map/ppermute | solution.py:19
  58.8 6.7 %collective-permute-start.4 = (f32[1,1,128,128]{3,2,1,0:T(8,128)}, f32[1,1,128,128]{3,2,1,0:T(8,128)S(1)}, u32[]{:S(2)}, u32[]{:S(2)}) collective-permute-start(f32[1,1,128,128]{3,2,1,0:T(8,128)} %get-tuple-element.23), channel_id=1, source_target_pairs={{0,1},{1,2},{2,3},{3,4},{4,5},{5,6},{6,7},{7,8},{8,9},{9,10},{10,1... | collective-permute-start | bytes 196616 | tf_op jit(solution)/shard_map/ppermute | solution.py:18
  66.0 0.8 copy-start
  67.0 17.3 %copy-start.2 = (f32[2,64,64]{2,1,0:T(8,128)S(1)}, f32[2,64,64]{2,1,0:T(8,128)}, u32[]{:S(2)}) copy-start(f32[2,64,64]{2,1,0:T(8,128)} %copy.20) | copy-start | bytes 98308
  67.0 17.3 %copy-start.1 = (f32[2,64,64]{2,1,0:T(8,128)S(1)}, f32[2,64,64]{2,1,0:T(8,128)}, u32[]{:S(2)}) copy-start(f32[2,64,64]{2,1,0:T(8,128)} %copy.21) | copy-start | bytes 98308
  67.0 1.2 collective-permute-start.10
  68.3 3.6 %collective-permute-start.11 = (f32[4,2]{0,1:T(2,128)S(1)}, f32[4,2]{0,1:T(2,128)S(1)}, u32[]{:S(2)}, u32[]{:S(2)}) collective-permute-start(f32[4,2]{0,1:T(2,128)S(1)} %maximum_select_fusion), channel_id=1, source_target_pairs={{0,2},{1,3},{2,0},{3,1},{4,6},{5,7},{6,4},{7,5},{8,10},{9,11},{10,... | collective-permute-start | bytes 104 | tf_op jit(solution)/shard_map/ppermute | solution.py:176
  72.0 3.6 %collective-permute-start.12 = (f32[8,2]{0,1:T(2,128)S(1)}, f32[8,2]{0,1:T(2,128)S(1)}, u32[]{:S(2)}, u32[]{:S(2)}) collective-permute-start(f32[8,2]{0,1:T(2,128)S(1)} %maximum_select_fusion.1), channel_id=1, source_target_pairs={{0,4},{1,5},{2,6},{3,7},{4,0},{5,1},{6,2},{7,3},{8,12},{9,13},{10,... | collective-permute-start | bytes 200 | tf_op jit(solution)/shard_map/ppermute | solution.py:176
  72.0 12.0 %collective-permute-start.7 = (f32[1,1,64,64]{3,2,1,0:T(8,128)S(1)}, f32[1,1,64,64]{3,2,1,0:T(8,128)S(1)}, u32[]{:S(2)}, u32[]{:S(2)}) collective-permute-start(f32[1,1,64,64]{3,2,1,0:T(8,128)S(1)} %get-tuple-element.40), channel_id=1, source_target_pairs={{1,0},{2,1},{3,2},{4,3},{5,4},{6,5},{7,6},{8,7},{9,8},{10,9},{11,1... | collective-permute-start | bytes 49160 | tf_op jit(solution)/shard_map/ppermute | solution.py:19
  75.6 4.5 %collective-permute-start.13 = (f32[16,2]{0,1:T(2,128)S(1)}, f32[16,2]{0,1:T(2,128)S(1)}, u32[]{:S(2)}, u32[]{:S(2)}) collective-permute-start(f32[16,2]{0,1:T(2,128)S(1)} %maximum_select_fusion.2), channel_id=1, source_target_pairs={{0,8},{1,9},{2,10},{3,11},{4,12},{5,13},{6,14},{7,15},{8,0},{9,1},... | collective-permute-start | bytes 392 | tf_op jit(solution)/shard_map/ppermute | solution.py:176
  78.2 6.1 %collective-permute-start.6 = (f32[1,1,64,64]{3,2,1,0:T(8,128)S(1)}, f32[1,1,64,64]{3,2,1,0:T(8,128)S(1)}, u32[]{:S(2)}, u32[]{:S(2)}) collective-permute-start(f32[1,1,64,64]{3,2,1,0:T(8,128)S(1)} %get-tuple-element.39), channel_id=1, source_target_pairs={{0,1},{1,2},{2,3},{3,4},{4,5},{5,6},{6,7},{7,8},{8,9},{9,10},{10,1... | collective-permute-start | bytes 49160 | tf_op jit(solution)/shard_map/ppermute | solution.py:18
  84.5 65.8 %collective-permute-start.9 = (f32[1,1,64,64]{3,2,1,0:T(8,128)S(1)}, f32[1,1,64,64]{3,2,1,0:T(8,128)S(1)}, u32[]{:S(2)}, u32[]{:S(2)}) collective-permute-start(f32[1,1,64,64]{3,2,1,0:T(8,128)S(1)} %get-tuple-element.36), channel_id=1, source_target_pairs={{1,0},{2,1},{3,2},{4,3},{5,4},{6,5},{7,6},{8,7},{9,8},{10,9},{11,1... | collective-permute-start | bytes 49160 | tf_op jit(solution)/shard_map/ppermute | solution.py:19
  88.7 61.6 %collective-permute-start.8 = (f32[1,1,64,64]{3,2,1,0:T(8,128)S(1)}, f32[1,1,64,64]{3,2,1,0:T(8,128)S(1)}, u32[]{:S(2)}, u32[]{:S(2)}) collective-permute-start(f32[1,1,64,64]{3,2,1,0:T(8,128)S(1)} %get-tuple-element.35), channel_id=1, source_target_pairs={{0,1},{1,2},{2,3},{3,4},{4,5},{5,6},{6,7},{7,8},{8,9},{9,10},{10,1... | collective-permute-start | bytes 49160 | tf_op jit(solution)/shard_map/ppermute | solution.py:18
  218.7 4.3 %collective-permute-start.15 = (f32[1,1,64,64]{3,2,1,0:T(8,128)S(1)}, f32[1,1,64,64]{3,2,1,0:T(8,128)S(1)}, u32[]{:S(2)}, u32[]{:S(2)}) collective-permute-start(f32[1,1,64,64]{3,2,1,0:T(8,128)S(1)} %get-tuple-element.32), channel_id=1, source_target_pairs={{1,0},{2,1},{3,2},{4,3},{5,4},{6,5},{7,6},{8,7},{9,8},{10,9},{11,1... | collective-permute-start | bytes 49160 | tf_op jit(solution)/shard_map/ppermute | solution.py:19
  220.6 6.1 %collective-permute-start.14 = (f32[1,1,64,64]{3,2,1,0:T(8,128)S(1)}, f32[1,1,64,64]{3,2,1,0:T(8,128)S(1)}, u32[]{:S(2)}, u32[]{:S(2)}) collective-permute-start(f32[1,1,64,64]{3,2,1,0:T(8,128)S(1)} %get-tuple-element.31), channel_id=1, source_target_pairs={{0,1},{1,2},{2,3},{3,4},{4,5},{5,6},{6,7},{7,8},{8,9},{9,10},{10,1... | collective-permute-start | bytes 49160 | tf_op jit(solution)/shard_map/ppermute | solution.py:18
  226.9 4.4 %collective-permute-start.17 = (f32[1,1,64,64]{3,2,1,0:T(8,128)S(1)}, f32[1,1,64,64]{3,2,1,0:T(8,128)S(1)}, u32[]{:S(2)}, u32[]{:S(2)}) collective-permute-start(f32[1,1,64,64]{3,2,1,0:T(8,128)S(1)} %get-tuple-element.30), channel_id=1, source_target_pairs={{1,0},{2,1},{3,2},{4,3},{5,4},{6,5},{7,6},{8,7},{9,8},{10,9},{11,1... | collective-permute-start | bytes 49160 | tf_op jit(solution)/shard_map/ppermute | solution.py:19
  229.4 6.9 %collective-permute-start.16 = (f32[1,1,64,64]{3,2,1,0:T(8,128)S(1)}, f32[1,1,64,64]{3,2,1,0:T(8,128)S(1)}, u32[]{:S(2)}, u32[]{:S(2)}) collective-permute-start(f32[1,1,64,64]{3,2,1,0:T(8,128)S(1)} %get-tuple-element.29), channel_id=1, source_target_pairs={{0,1},{1,2},{2,3},{3,4},{4,5},{5,6},{6,7},{7,8},{8,9},{9,10},{10,1... | collective-permute-start | bytes 49160 | tf_op jit(solution)/shard_map/ppermute | solution.py:18
  236.7 4.3 %collective-permute-start.19 = (f32[1,1,128,128]{3,2,1,0:T(8,128)S(1)}, f32[1,1,128,128]{3,2,1,0:T(8,128)S(1)}, u32[]{:S(2)}, u32[]{:S(2)}) collective-permute-start(f32[1,1,128,128]{3,2,1,0:T(8,128)S(1)} %get-tuple-element.22), channel_id=1, source_target_pairs={{1,0},{2,1},{3,2},{4,3},{5,4},{6,5},{7,6},{8,7},{9,8},{10,9},{11,1... | collective-permute-start | bytes 196616 | tf_op jit(solution)/shard_map/ppermute | solution.py:19
  238.7 6.5 %collective-permute-start.18 = (f32[1,1,128,128]{3,2,1,0:T(8,128)S(1)}, f32[1,1,128,128]{3,2,1,0:T(8,128)S(1)}, u32[]{:S(2)}, u32[]{:S(2)}) collective-permute-start(f32[1,1,128,128]{3,2,1,0:T(8,128)S(1)} %get-tuple-element.21), channel_id=1, source_target_pairs={{0,1},{1,2},{2,3},{3,4},{4,5},{5,6},{6,7},{7,8},{8,9},{9,10},{10,1... | collective-permute-start | bytes 196616 | tf_op jit(solution)/shard_map/ppermute | solution.py:18
  245.6 4.3 %collective-permute-start.21 = (f32[1,1,128,128]{3,2,1,0:T(8,128)S(1)}, f32[1,1,128,128]{3,2,1,0:T(8,128)S(1)}, u32[]{:S(2)}, u32[]{:S(2)}) collective-permute-start(f32[1,1,128,128]{3,2,1,0:T(8,128)S(1)} %get-tuple-element.20), channel_id=1, source_target_pairs={{1,0},{2,1},{3,2},{4,3},{5,4},{6,5},{7,6},{8,7},{9,8},{10,9},{11,1... | collective-permute-start | bytes 196616 | tf_op jit(solution)/shard_map/ppermute | solution.py:19
  247.5 6.5 %collective-permute-start.20 = (f32[1,1,128,128]{3,2,1,0:T(8,128)S(1)}, f32[1,1,128,128]{3,2,1,0:T(8,128)S(1)}, u32[]{:S(2)}, u32[]{:S(2)}) collective-permute-start(f32[1,1,128,128]{3,2,1,0:T(8,128)S(1)} %get-tuple-element.19), channel_id=1, source_target_pairs={{0,1},{1,2},{2,3},{3,4},{4,5},{5,6},{6,7},{7,8},{8,9},{9,10},{10,1... | collective-permute-start | bytes 196616 | tf_op jit(solution)/shard_map/ppermute | solution.py:18
